TPU v7x, 32 devices: a whole 2x2x4 slice. The times are simulated.
32 devices in a mesh: groups: 2 (over x), seq: 16 (over z, y, core).
Axes of the slice: x: 2, y: 2, z: 4, core: 2. Of those that a mesh axis runs over, the one named last changes fastest.
Arguments:
- queries: bfloat16 [256, 2560], P(('groups', 'seq')), parts along dimension 0, may hold values from -160 to 160
- new_keys: bfloat16 [256, 2560], P(('groups', 'seq')), parts along dimension 0, may hold values from -7 to 7
- new_values: bfloat16 [256, 2560], P(('groups', 'seq')), parts along dimension 0, may hold values from -6 to 6
- cache_keys: bfloat16 [16384, 2560], P(('groups', 'seq')), parts along dimension 0, may hold values from -6 to 6
- cache_values: bfloat16 [16384, 2560], P(('groups', 'seq')), parts along dimension 0, may hold values from -6 to 6
- victims: int32 [32], P('groups'), parts along dimension 0, may hold values from 0 to 63, as said below
Outputs:
- attended: bfloat16 [256, 2560], P(('groups', 'seq')), parts along dimension 0
There are 2 independent parts, one for each index of `groups`. A program takes and returns all parts, laid end to end along the dimension named above; each array names one. Nothing has to cross between parts.
Inputs may be any that keep to these rules, and one draw needn't show every extreme that they name: `victims`: 16 distinct block ids of the cache; the first and the last block are always among them.
All inputs are finite; a program needn't handle non-finite values.
Results may differ from a plain program's by a relative error of at most 0.01.
Values may be sent and summed in bfloat16 or wider, within the bound.
A program may use at most 128 MiB of HBM per device.

v0:
```python
import functools
import math

import jax
import jax.numpy as jnp
from jax import lax
from jax.experimental import pallas as pl
from jax.experimental.pallas import tpu as pltpu
from jax.sharding import PartitionSpec as P

HD = 128
BLK = 128
LANES = 128
HALF = 32
ROW_TILE = 128
OFFSETS = (0.0, 5.0, 7.3, 9.0, 12.0, 16.0)
STEP = 5.0


def factors(members):
    fc = 2 if members % 2 == 0 else 1
    rest = members // fc
    fa = rest
    for cand in range(1, rest + 1):
        if rest % cand == 0 and cand * cand >= rest:
            fa = cand
            break
    return fa, rest // fa, fc


def chunks_of(heads):
    for count in (4, 5, 2, 3):
        if heads % count == 0 and heads // count <= HALF:
            return count
    return 1 if heads <= HALF else heads


def kernel(
    dims, chunks, q_hbm, nk_hbm, nv_hbm, vic_hbm, ck_ref, cv_ref, o_ref,
    nk_ref, nv_ref, vic_ref, qall, kbuf, vbuf, acc, send_c, recv_c, send_b, recv_b, send_a, recv_a,
    load_sem, small_sem, gs_sem, gr_sem, rs_sem, rr_sem,
):
    fa, fb, fc = dims
    members = fa * fb * fc
    tok, columns = q_hbm.shape
    heads = columns // HD
    hc = heads // chunks
    width = hc * HD
    wide = width + LANES
    rows = ck_ref.shape[0]
    keys = kbuf.shape[0]
    block_count = rows // BLK
    exponent = math.log2(math.e) / math.sqrt(HD)

    me = lax.axis_index("seq")
    c = lax.rem(me, fc)
    b = lax.rem(lax.div(me, fc), fb)
    a = lax.div(me, fc * fb)

    def index(a_, b_, c_):
        return (a_ * fb + b_) * fc + c_

    def slot(a_, b_, c_):
        return (c_ * fb + b_) * fa + a_

    def partners(x, size):
        if size & (size - 1):
            return [lax.rem(x + d, size) for d in range(1, size)], [
                lax.rem(x + size - d, size) for d in range(1, size)
            ]
        found = []
        for d in range(1, size):
            y = x
            bit = 1
            while bit <= d:
                if d & bit:
                    y = y + bit - 2 * bit * lax.rem(lax.div(y, bit), 2)
                bit *= 2
            found.append(y)
        return found, found

    a_peers, a_from = partners(a, fa)
    b_peers, b_from = partners(b, fb)
    c_peers, c_from = partners(c, fc)
    devices = (
        [index(p, b, c) for p in a_peers]
        + [index(a, p, c) for p in b_peers]
        + [index(a, b, p) for p in c_peers]
    )
    na, nb, nc = fa - 1, fb - 1, fc - 1

    def cols(j):
        return pl.ds(j * width, width)

    def wcols(j):
        return pl.ds(j * wide, wide)

    barrier = pltpu.get_barrier_semaphore()
    for dev in devices:
        pl.semaphore_signal(
            barrier, inc=1, device_id={"seq": dev}, device_id_type=pl.DeviceIdType.MESH
        )

    loads = []
    for j in range(chunks):
        pair = (
            pltpu.make_async_copy(
                ck_ref.at[:, cols(j)], kbuf.at[pl.ds(0, rows), cols(j)], load_sem.at[j, 0]
            ),
            pltpu.make_async_copy(
                cv_ref.at[:, cols(j)], vbuf.at[pl.ds(0, rows), cols(j)], load_sem.at[j, 1]
            ),
        )
        loads.append(pair)
    own_slot = slot(a, b, c)
    own = pltpu.make_async_copy(q_hbm, qall.at[own_slot], small_sem.at[0])
    small = [
        pltpu.make_async_copy(nk_hbm, nk_ref, small_sem.at[1]),
        pltpu.make_async_copy(nv_hbm, nv_ref, small_sem.at[2]),
        pltpu.make_async_copy(vic_hbm, vic_ref, small_sem.at[3]),
    ]
    own.start()
    for copy in small:
        copy.start()
    for pair in loads:
        pair[0].start()
        pair[1].start()

    def remote(src, dst, sems, recvs, j, k, target):
        return pltpu.make_async_remote_copy(
            src_ref=src,
            dst_ref=dst,
            send_sem=sems.at[j, k],
            recv_sem=recvs.at[j, k],
            device_id={"seq": target},
            device_id_type=pl.DeviceIdType.MESH,
        )

    def gather(src, j, k, target):
        return remote(src, src, gs_sem, gr_sem, j, k, target)

    def gather_a(j):
        src = qall.at[own_slot, :, cols(j)]
        return [gather(src, j, k, devices[k]) for k in range(na)]

    def gather_b(j, source):
        block = own_slot if source == 0 else slot(a_from[source - 1], b, c)
        src = qall.at[block, :, cols(j)]
        return [gather(src, j, na + source * nb + k, devices[na + k]) for k in range(nb)]

    def gather_c(j, column):
        at_b = b if column == 0 else b_from[column - 1]
        src = qall.at[pl.ds(slot(0, at_b, c), fa), :, cols(j)]
        return [
            gather(src, j, na + fa * nb + column * nc + k, devices[na + nb + k]) for k in range(nc)
        ]

    own.wait()
    pl.semaphore_wait(barrier, len(devices))
    for j in range(chunks):
        for copy in gather_a(j):
            copy.start()
        for copy in gather_b(j, 0):
            copy.start()
    for copy in small:
        copy.wait()

    pad16 = 2 * tok - tok
    for src, dst in ((nk_ref, kbuf), (nv_ref, vbuf)):
        fresh = src[...].astype(jnp.float32)
        dst[pl.ds(rows, 2 * tok), :] = jnp.concatenate(
            [fresh, jnp.zeros((pad16, columns), jnp.float32)], axis=0
        ).astype(jnp.bfloat16)
        dst[pl.ds(rows + 2 * tok, keys - rows - 2 * tok), :] = jnp.zeros(
            (keys - rows - 2 * tok, columns), jnp.bfloat16
        )

    victims = vic_ref[...]
    pieces = []
    for k in range(block_count):
        hit = jnp.where(victims == me * block_count + k, 1.0, 0.0)
        hit = jnp.max(hit, axis=1, keepdims=True)
        pieces.append(jnp.broadcast_to(hit, (1, BLK)) * -1e30)
    tail = lax.broadcasted_iota(jnp.int32, (1, keys - rows), 1)
    pieces.append(jnp.where(tail < tok, 0.0, -1e30))
    bias = jnp.concatenate(pieces, axis=1)

    tile_slots = max(1, min(members, ROW_TILE // tok))
    tiles = members // tile_slots

    def lane_of(r):
        return lax.broadcasted_iota(jnp.int32, (r, LANES), 1)

    def compute(j):
        def tile(t):
            first = t * tile_slots
            r = tile_slots * tok
            lane = lane_of(r)

            def scores(h):
                col = j * width + h * HD
                col = col if isinstance(col, int) else pl.multiple_of(col, HD)
                q = qall[pl.ds(first, tile_slots), :, pl.ds(col, HD)]
                q = q.astype(jnp.float32).reshape(r, HD).astype(jnp.bfloat16)
                return lax.dot_general(
                    q, kbuf[:, pl.ds(col, HD)], (((1,), (1,)), ((), ())),
                    preferred_element_type=jnp.float32,
                )

            def head(h, stats, s):
                col = j * width + h * HD
                col = col if isinstance(col, int) else pl.multiple_of(col, HD)
                s = s * exponent + bias
                top = jnp.max(s, axis=1, keepdims=True)
                top = top.astype(jnp.bfloat16).astype(jnp.float32)
                e = jnp.exp2(s - top)
                mass = jnp.sum(e, axis=1, keepdims=True)
                out = jnp.dot(
                    e.astype(jnp.bfloat16), vbuf[:, pl.ds(col, HD)],
                    preferred_element_type=jnp.float32,
                )
                at = j * wide + h * HD
                at = at if isinstance(at, int) else pl.multiple_of(at, HD)
                acc[pl.ds(first, tile_slots), :, pl.ds(at, HD)] = out.reshape(tile_slots, tok, HD)
                stats = jnp.where(lane == h, top, stats)
                return jnp.where(lane == h + HALF, mass, stats)

            stats = jnp.zeros((r, LANES), jnp.float32)
            if tiles == 1:
                ahead = scores(0)
                for h in range(hc):
                    now, ahead = ahead, scores(h + 1) if h + 1 < hc else None
                    stats = head(h, stats, now)
            else:
                stats = lax.fori_loop(0, hc, lambda h, st: head(h, st, scores(h)), stats)
            acc[pl.ds(first, tile_slots), :, pl.ds(j * wide + width, LANES)] = stats.reshape(
                tile_slots, tok, LANES
            )

        if tiles == 1:
            tile(0)
        else:
            pl.loop(0, tiles)(tile)

    def encode(stats):
        high = stats.astype(jnp.bfloat16).astype(jnp.float32)
        return (high + pltpu.roll(stats - high, HALF, 1)).astype(jnp.bfloat16)

    def decode(stats):
        low = pltpu.roll(stats, LANES - HALF, 1)
        return stats + jnp.where(lane_of(stats.shape[0]) < HALF, 0.0, low)

    def pack(first, count, buf, j):
        r = count * tok
        buf[:, :, cols_w(j, width)] = acc[pl.ds(first, count), :, cols_w(j, width)].astype(
            jnp.bfloat16
        )
        stats = acc[pl.ds(first, count), :, pl.ds(j * wide + width, LANES)].reshape(r, LANES)
        buf[:, :, pl.ds(j * wide + width, LANES)] = encode(stats).reshape(count, tok, LANES)

    def cols_w(j, w):
        return pl.ds(j * wide, w)

    def merge(first, count, parts, j, last=False):
        r = count * tok
        at = pl.ds(j * wide + width, LANES)
        lane = lane_of(r)
        stats = [acc[pl.ds(first, count), :, at].reshape(r, LANES)]
        for ref in parts:
            stats.append(decode(ref[:, :, at].astype(jnp.float32).reshape(r, LANES)))
        top = functools.reduce(jnp.maximum, stats)
        factor = [jnp.exp2(s - top) for s in stats]
        mass = sum(pltpu.roll(f, HALF, 1) * s for f, s in zip(factor, stats))
        if last:
            inverse = pltpu.roll(1.0 / jnp.where(lane < HALF, 1.0, mass), LANES - HALF, 1)
            factor = [f * inverse for f in factor]
        for h in range(hc):
            here = pl.ds(j * wide + h * HD, HD)
            total = acc[pl.ds(first, count), :, here].reshape(r, HD) * factor[0][:, h : h + 1]
            for f, ref in zip(factor[1:], parts):
                total = total + ref[:, :, here].astype(jnp.float32).reshape(r, HD) * f[:, h : h + 1]
            if last:
                o_ref[:, pl.ds(j * width + h * HD, HD)] = total.astype(jnp.bfloat16)
            else:
                acc[pl.ds(first, count), :, here] = total.reshape(count, tok, HD)
        if not last:
            fused = jnp.where(lane < HALF, top, jnp.where(lane < 2 * HALF, mass, 0.0))
            acc[pl.ds(first, count), :, at] = fused.reshape(count, tok, LANES)

    def scatter_c(j):
        return [
            remote(
                send_c.at[k, :, :, wcols(j)], recv_c.at[k, :, :, wcols(j)], rs_sem, rr_sem, j, na + nb + k,
                devices[na + nb + k],
            )
            for k in range(nc)
        ]

    def scatter_b(j):
        return [
            remote(
                send_b.at[k, :, :, wcols(j)], recv_b.at[k, :, :, wcols(j)], rs_sem, rr_sem, j, na + k,
                devices[na + k],
            )
            for k in range(nb)
        ]

    def scatter_a(j):
        return [
            remote(
                send_a.at[k, :, :, wcols(j)], recv_a.at[k, :, :, wcols(j)], rs_sem, rr_sem, j, k,
                devices[k],
            )
            for k in range(na)
        ]

    def stage_0(j):
        for source in range(1, fa):
            gather_a(j)[source - 1].wait_recv()
            for copy in gather_b(j, source):
                copy.start()
        for copy in gather_c(j, 0):
            copy.start()

    def stage_1(j):
        for column in range(1, fb):
            for source in range(fa):
                gather_b(j, source)[column - 1].wait_recv()
            for copy in gather_c(j, column):
                copy.start()

    def stage_2(j):
        for column in range(fb):
            for copy in gather_c(j, column):
                copy.wait_recv()
        for copy in loads[j]:
            copy.wait()
        compute(j)
        for k, copy in enumerate(scatter_c(j)):
            pack(slot(0, 0, c_peers[k]), fa * fb, send_c.at[k], j)
            copy.start()

    def stage_3(j):
        for copy in scatter_c(j):
            copy.wait_recv()
        received = [recv_c.at[k] for k in range(nc)]
        for k, copy in enumerate(scatter_b(j)):
            first = b_peers[k] * fa
            merge(slot(0, b_peers[k], c), fa, [x.at[pl.ds(first, fa)] for x in received], j)
            pack(slot(0, b_peers[k], c), fa, send_b.at[k], j)
            copy.start()
        merge(slot(0, b, c), fa, [x.at[pl.ds(b * fa, fa)] for x in received], j)

    def stage_4(j):
        for copy in scatter_b(j):
            copy.wait_recv()
        merge(slot(0, b, c), fa, [recv_b.at[k] for k in range(nb)], j)
        for k, copy in enumerate(scatter_a(j)):
            pack(slot(a_peers[k], b, c), 1, send_a.at[k], j)
            copy.start()

    def stage_5(j):
        for copy in scatter_a(j):
            copy.wait_recv()
        merge(own_slot, 1, [recv_a.at[k] for k in range(na)], j, last=True)

    stages = (stage_0, stage_1, stage_2, stage_3, stage_4, stage_5)
    order = sorted(
        (OFFSETS[number] + j * STEP / chunks, number, j)
        for number in range(len(stages))
        for j in range(chunks)
    )
    for _, number, j in order:
        stages[number](j)
    for j in range(chunks):
        groups = [gather_a(j), scatter_a(j), scatter_b(j), scatter_c(j)]
        groups += [gather_b(j, source) for source in range(fa)]
        groups += [gather_c(j, column) for column in range(fb)]
        for group in groups:
            for copy in group:
                copy.wait_send()


def per_device(queries, new_keys, new_values, cache_keys, cache_values, victims):
    members = lax.axis_size("seq")
    dims = fa, fb, fc = factors(members)
    tok, columns = queries.shape
    heads = columns // HD
    chunks = chunks_of(heads)
    rows = cache_keys.shape[0]
    keys = rows + -(-2 * tok // LANES) * LANES
    total = columns + chunks * LANES
    peers = fa + fb + fc - 3
    copies = fa - 1 + fa * (fb - 1) + fb * (fc - 1)
    bf16 = jnp.bfloat16
    vmem = pl.BlockSpec(memory_space=pltpu.VMEM)
    hbm = pl.BlockSpec(memory_space=pl.ANY)
    return pl.pallas_call(
        functools.partial(kernel, dims, chunks),
        out_shape=jax.ShapeDtypeStruct((tok, columns), bf16),
        in_specs=[hbm] * 6,
        out_specs=vmem,
        scratch_shapes=[
            pltpu.VMEM((tok, columns), bf16),
            pltpu.VMEM((tok, columns), bf16),
            pltpu.VMEM((1, victims.shape[0]), jnp.int32),
            pltpu.VMEM((members, tok, columns), bf16),
            pltpu.VMEM((keys, columns), bf16),
            pltpu.VMEM((keys, columns), bf16),
            pltpu.VMEM((members, tok, total), jnp.float32),
            pltpu.VMEM((max(1, fc - 1), fa * fb, tok, total), bf16),
            pltpu.VMEM((max(1, fc - 1), fa * fb, tok, total), bf16),
            pltpu.VMEM((max(1, fb - 1), fa, tok, total), bf16),
            pltpu.VMEM((max(1, fb - 1), fa, tok, total), bf16),
            pltpu.VMEM((max(1, fa - 1), 1, tok, total), bf16),
            pltpu.VMEM((max(1, fa - 1), 1, tok, total), bf16),
            pltpu.SemaphoreType.DMA((chunks, 2)),
            pltpu.SemaphoreType.DMA((4,)),
            pltpu.SemaphoreType.DMA((chunks, copies)),
            pltpu.SemaphoreType.DMA((chunks, copies)),
            pltpu.SemaphoreType.DMA((chunks, peers)),
            pltpu.SemaphoreType.DMA((chunks, peers)),
        ],
        compiler_params=pltpu.CompilerParams(
            collective_id=0, has_side_effects=True, vmem_limit_bytes=60 * 1024 * 1024
        ),
    )(queries, new_keys, new_values, victims.reshape(1, -1), cache_keys, cache_values)


def solution(mesh):
    row = P(("groups", "seq"), None)
    return jax.shard_map(
        per_device,
        mesh=mesh,
        in_specs=(row, row, row, row, row, P("groups")),
        out_specs=row,
        check_vma=False,
    )
```

profile of v0, /device:TPU:0, one launch (start us, length us, event | category | flops | bytes accessed | tf_op | source)
XLA Modules:
  0.0 30.4 jit_solution(16119428136172952520)
XLA Ops:
  0.0 28.9 %shard_map.64 = bf16[8,2560]{1,0:T(8,128)(2,1)} custom-call(bf16[8,2560]{1,0:T(8,128)(2,1)} %q_hbm.1, bf16[8,2560]{1,0:T(8,128)(2,1)} %nk_hbm.1, bf16[8,2560]{1,0:T(8,128)(2,1)} %nv_hbm.1, s32[1,16]{1,0:T(1,128)} %bitcast.1, bf16[512,2560]{1,0:T(8,128)(2,1)} %ck_ref.1, bf16[512,2560]{1,0:T(8,128)(2,1)} %cv_ref.1), custom_call_target="tpu_custom_call" | custom-call | tf_op jit(solution)/shard_map/pallas_call | solution.py:398
  29.0 1.4 %copy.8 = bf16[8,2560]{1,0:T(8,128)(2,1)} copy(bf16[8,2560]{1,0:T(8,128)(2,1)} %shard_map.64) | data formatting | bytes 81920
where the time goes:
time: 30.5 us; the launch traced here: 30.4 us
  Pallas kernels  28.9 us (95%)
  local copies, waits for them, and re-layouts  1.4 us (5%)
    pallas_call x1, Pallas kernels, per_device(): pl.pallas_call(functools.partial(kernel, dims, chunks), out_shape=jax.Sha...  28.9 us
    unnamed x1, local copies, waits for them, and re-layouts  1.4 us

commit v1 on v0

v1 whole, which is shorter than its diff:
```python
import functools
import math

import jax
import jax.numpy as jnp
from jax import lax
from jax.experimental import pallas as pl
from jax.experimental.pallas import tpu as pltpu
from jax.sharding import PartitionSpec as P

HD = 128
BLK = 128
LANES = 128
HALF = 32
ROW_TILE = 128
SIZES = (4, 6, 6, 4)
GROUPS = ((0, 1), (1, 2), (2, 4))
ORDER = ((0, 0), (0, 1), (0, 2), (1, 0), (1, 1), (2, 0), (1, 2), (2, 1), (3, 0), (2, 2), (3, 1), (2, 3), (3, 2), (4, 0), (3, 3), (4, 1), (4, 2), (4, 3), (5, 0), (5, 1), (5, 2), (5, 3))


def factors(members):
    fc = 2 if members % 2 == 0 else 1
    rest = members // fc
    fa = rest
    for cand in range(1, rest + 1):
        if rest % cand == 0 and cand * cand >= rest:
            fa = cand
            break
    return fa, rest // fa, fc


def chunks_of(heads):
    return SIZES


def kernel(
    dims, sizes, q_hbm, nk_hbm, nv_hbm, vic_hbm, ck_ref, cv_ref, o_ref,
    nk_ref, nv_ref, vic_ref, qall, kbuf, vbuf, live, acc, send_c, recv_c, send_b, recv_b, send_a, recv_a,
    load_sem, small_sem, send_sem, ga_sem, gb_sem, gc_sem, rr_sem,
):
    fa, fb, fc = dims
    members = fa * fb * fc
    tok, columns = q_hbm.shape
    heads = columns // HD
    chunks = len(sizes)
    starts = [sum(sizes[:j]) * HD for j in range(chunks + 1)]
    rows = ck_ref.shape[0]
    keys = kbuf.shape[0]
    block_count = rows // BLK
    exponent = math.log2(math.e) / math.sqrt(HD)

    me = lax.axis_index("seq")
    c = lax.rem(me, fc)
    b = lax.rem(lax.div(me, fc), fb)
    a = lax.div(me, fc * fb)

    def index(a_, b_, c_):
        return (a_ * fb + b_) * fc + c_

    def slot(a_, b_, c_):
        return (c_ * fb + b_) * fa + a_

    def partners(x, size):
        if size & (size - 1):
            return [lax.rem(x + d, size) for d in range(1, size)], [
                lax.rem(x + size - d, size) for d in range(1, size)
            ]
        found = []
        for d in reversed(range(1, size)):
            y = x
            bit = 1
            while bit <= d:
                if d & bit:
                    y = y + bit - 2 * bit * lax.rem(lax.div(y, bit), 2)
                bit *= 2
            found.append(y)
        return found, found

    a_peers, a_from = partners(a, fa)
    b_peers, b_from = partners(b, fb)
    c_peers, c_from = partners(c, fc)
    devices = (
        [index(p, b, c) for p in a_peers]
        + [index(a, p, c) for p in b_peers]
        + [index(a, b, p) for p in c_peers]
    )
    na, nb, nc = fa - 1, fb - 1, fc - 1

    def cols(g):
        low, high = GROUPS[g]
        return pl.ds(starts[low], starts[high] - starts[low])

    def packed(j, h=0):
        return starts[j] + j * LANES + h * HD

    def stat(j):
        return pl.ds(packed(j, sizes[j]), LANES)

    def body(j):
        return pl.ds(packed(j), sizes[j] * HD)

    def wcols(j):
        return pl.ds(packed(j), sizes[j] * HD + LANES)

    barrier = pltpu.get_barrier_semaphore()
    for dev in devices:
        pl.semaphore_signal(
            barrier, inc=1, device_id={"seq": dev}, device_id_type=pl.DeviceIdType.MESH
        )

    loads = [
        pltpu.make_async_copy(src, dst.at[pl.ds(0, rows)], load_sem.at[k])
        for k, (src, dst) in enumerate(((ck_ref, kbuf), (cv_ref, vbuf)))
    ]
    own_slot = slot(a, b, c)
    own = pltpu.make_async_copy(q_hbm, qall.at[own_slot], small_sem.at[0])
    small = [
        pltpu.make_async_copy(nk_hbm, nk_ref, small_sem.at[1]),
        pltpu.make_async_copy(nv_hbm, nv_ref, small_sem.at[2]),
        pltpu.make_async_copy(vic_hbm, vic_ref, small_sem.at[3]),
    ]
    own.start()
    for copy in small:
        copy.start()
    for copy in loads:
        copy.start()

    def remote(src, dst, out, into, target):
        return pltpu.make_async_remote_copy(
            src_ref=src,
            dst_ref=dst,
            send_sem=send_sem.at[out],
            recv_sem=into,
            device_id={"seq": target},
            device_id_type=pl.DeviceIdType.MESH,
        )

    def arrived(ref, sem):
        pltpu.make_async_copy(ref, ref, sem).wait()

    def gather_a(j):
        src = qall.at[own_slot, :, cols(j)]
        return [remote(src, src, 0, ga_sem.at[j, k], devices[k]) for k in range(na)]

    def gather_b(j, source):
        block = own_slot if source == 0 else slot(a_from[source - 1], b, c)
        src = qall.at[block, :, cols(j)]
        return [remote(src, src, 1, gb_sem.at[j, k], devices[na + k]) for k in range(nb)]

    def gather_c(j, column):
        at_b = b if column == 0 else b_from[column - 1]
        src = qall.at[pl.ds(slot(0, at_b, c), fa), :, cols(j)]
        return [remote(src, src, 2, gc_sem.at[j], devices[na + nb + k]) for k in range(nc)]

    with jax.named_scope('bar'):
        own.wait()
        pl.semaphore_wait(barrier, len(devices))
    for j in range(len(GROUPS)):
        for copy in gather_a(j):
            copy.start()
        for copy in gather_b(j, 0):
            copy.start()
    for copy in small:
        copy.wait()

    fresh = nk_ref[...].astype(jnp.float32)
    spare = jnp.concatenate([fresh, fresh], axis=0).astype(jnp.bfloat16)
    fresh = nv_ref[...].astype(jnp.float32)
    value = jnp.concatenate([fresh, jnp.zeros_like(fresh)], axis=0).astype(jnp.bfloat16)
    step = 2 * tok
    none = jnp.zeros((step, columns), jnp.bfloat16)
    first = lax.broadcasted_iota(jnp.int32, (step, LANES), 0)
    for at in range(rows, keys, step):
        here = pl.ds(at, step)
        kbuf[here, :] = spare
        vbuf[here, :] = value if at == rows else none
        live[here, :] = jnp.where(first < (tok if at == rows else 0), 1.0, 0.0).astype(jnp.bfloat16)

    victims = vic_ref[...]
    for copy in loads:
        copy.wait()
    for k in range(block_count):
        hit = jnp.where(victims == me * block_count + k, 1.0, 0.0)
        hit = jnp.max(hit, axis=1, keepdims=True)
        live[pl.ds(k * BLK, BLK), :] = jnp.broadcast_to(1.0 - hit, (BLK, LANES)).astype(jnp.bfloat16)
        gone = jnp.broadcast_to(hit, (step, LANES)) > 0.5

        @pl.loop(0, BLK // step)
        def _(r):
            here = pl.ds(pl.multiple_of(k * BLK + r * step, step), step)
            for col in range(0, columns, LANES):
                lanes = pl.ds(col, LANES)
                kbuf[here, lanes] = jnp.where(gone, spare[:, col : col + LANES], kbuf[here, lanes])
                vbuf[here, lanes] = jnp.where(gone, none[:, :LANES], vbuf[here, lanes])

    tile_slots = max(1, min(members, ROW_TILE // tok))
    tiles = members // tile_slots

    def lane_of(r):
        return lax.broadcasted_iota(jnp.int32, (r, LANES), 1)

    def compute(j):
        def tile(t):
            first = t * tile_slots
            r = tile_slots * tok
            lane = lane_of(r)

            def scores(h):
                col = starts[j] + h * HD
                col = col if isinstance(col, int) else pl.multiple_of(col, HD)
                q = qall[pl.ds(first, tile_slots), :, pl.ds(col, HD)]
                q = q.astype(jnp.float32).reshape(r, HD).astype(jnp.bfloat16)
                return lax.dot_general(
                    q, kbuf[:, pl.ds(col, HD)], (((1,), (1,)), ((), ())),
                    preferred_element_type=jnp.float32,
                )

            def head(h, stats, s):
                col = starts[j] + h * HD
                col = col if isinstance(col, int) else pl.multiple_of(col, HD)
                top = jnp.max(s, axis=1, keepdims=True) * exponent
                top = top.astype(jnp.bfloat16).astype(jnp.float32)
                e = jnp.exp2(s * exponent - top)
                out = jnp.dot(
                    e.astype(jnp.bfloat16),
                    jnp.concatenate([vbuf[:, pl.ds(col, HD)], live[...]], axis=1),
                    preferred_element_type=jnp.float32,
                )
                out, mass = out[:, :HD], out[:, HD:]
                at = packed(j) + h * HD
                at = at if isinstance(at, int) else pl.multiple_of(at, HD)
                acc[pl.ds(first, tile_slots), :, pl.ds(at, HD)] = out.reshape(tile_slots, tok, HD)
                stats = jnp.where(lane == h, top, stats)
                return jnp.where(lane == h + HALF, mass, stats)

            stats = jnp.zeros((r, LANES), jnp.float32)
            if tiles == 1:
                ahead = scores(0)
                for h in range(sizes[j]):
                    now, ahead = ahead, scores(h + 1) if h + 1 < sizes[j] else None
                    stats = head(h, stats, now)
            else:
                stats = lax.fori_loop(0, sizes[j], lambda h, st: head(h, st, scores(h)), stats)
            acc[pl.ds(first, tile_slots), :, stat(j)] = stats.reshape(
                tile_slots, tok, LANES
            )

        if tiles == 1:
            tile(0)
        else:
            pl.loop(0, tiles)(tile)

    def encode(stats):
        high = stats.astype(jnp.bfloat16).astype(jnp.float32)
        return (high + pltpu.roll(stats - high, HALF, 1)).astype(jnp.bfloat16)

    def decode(stats):
        low = pltpu.roll(stats, LANES - HALF, 1)
        return stats + jnp.where(lane_of(stats.shape[0]) < HALF, 0.0, low)

    def pack(first, count, buf, j):
        r = count * tok
        buf[:, :, body(j)] = acc[pl.ds(first, count), :, body(j)].astype(jnp.bfloat16)
        stats = acc[pl.ds(first, count), :, stat(j)].reshape(r, LANES)
        buf[:, :, stat(j)] = encode(stats).reshape(count, tok, LANES)

    def merge(first, count, parts, j, last=False):
        r = count * tok
        at = stat(j)
        lane = lane_of(r)
        stats = [acc[pl.ds(first, count), :, at].reshape(r, LANES)]
        for ref in parts:
            stats.append(decode(ref[:, :, at].astype(jnp.float32).reshape(r, LANES)))
        top = functools.reduce(jnp.maximum, stats)
        factor = [jnp.exp2(s - top) for s in stats]
        mass = sum(pltpu.roll(f, HALF, 1) * s for f, s in zip(factor, stats))
        if last:
            inverse = pltpu.roll(1.0 / jnp.where(lane < HALF, 1.0, mass), LANES - HALF, 1)
            factor = [f * inverse for f in factor]
        for h in range(sizes[j]):
            here = pl.ds(packed(j, h), HD)
            total = acc[pl.ds(first, count), :, here].reshape(r, HD) * factor[0][:, h : h + 1]
            for f, ref in zip(factor[1:], parts):
                total = total + ref[:, :, here].astype(jnp.float32).reshape(r, HD) * f[:, h : h + 1]
            if last:
                o_ref[:, pl.ds(starts[j] + h * HD, HD)] = total.astype(jnp.bfloat16)
            else:
                acc[pl.ds(first, count), :, here] = total.reshape(count, tok, HD)
        if not last:
            fused = jnp.where(lane < HALF, top, jnp.where(lane < 2 * HALF, mass, 0.0))
            acc[pl.ds(first, count), :, at] = fused.reshape(count, tok, LANES)

    def scatter_c(j):
        return [
            remote(
                send_c.at[k, :, :, wcols(j)], recv_c.at[k, :, :, wcols(j)], 5, rr_sem.at[j, 2],
                devices[na + nb + k],
            )
            for k in range(nc)
        ]

    def scatter_b(j):
        return [
            remote(
                send_b.at[k, :, :, wcols(j)], recv_b.at[k, :, :, wcols(j)], 4, rr_sem.at[j, 1],
                devices[na + k],
            )
            for k in range(nb)
        ]

    def scatter_a(j):
        return [
            remote(
                send_a.at[k, :, :, wcols(j)], recv_a.at[k, :, :, wcols(j)], 3, rr_sem.at[j, 0],
                devices[k],
            )
            for k in range(na)
        ]

    def stage_0(j):
        for source in range(1, fa):
            gather_a(j)[source - 1].wait_recv()
            for copy in gather_b(j, source):
                copy.start()
        for copy in gather_c(j, 0):
            copy.start()

    def stage_1(j):
        for column in range(1, fb):
            arrived(qall.at[pl.ds(0, fa), :, cols(j)], gb_sem.at[j, column - 1])
            for copy in gather_c(j, column):
                copy.start()

    def stage_2(j):
        for g, (low, _) in enumerate(GROUPS):
            if nc and low == j:
                arrived(qall.at[pl.ds(0, nc * fa * fb), :, cols(g)], gc_sem.at[g])
        compute(j)
        for k, copy in enumerate(scatter_c(j)):
            pack(slot(0, 0, c_peers[k]), fa * fb, send_c.at[k], j)
            copy.start()

    def stage_3(j):
        if nc:
            arrived(recv_c.at[:, :, :, wcols(j)], rr_sem.at[j, 2])
        received = [recv_c.at[k] for k in range(nc)]
        for k, copy in enumerate(scatter_b(j)):
            first = b_peers[k] * fa
            merge(slot(0, b_peers[k], c), fa, [x.at[pl.ds(first, fa)] for x in received], j)
            pack(slot(0, b_peers[k], c), fa, send_b.at[k], j)
            copy.start()
        merge(slot(0, b, c), fa, [x.at[pl.ds(b * fa, fa)] for x in received], j)

    def stage_4(j):
        if nb:
            arrived(recv_b.at[:, :, :, wcols(j)], rr_sem.at[j, 1])
        merge(slot(0, b, c), fa, [recv_b.at[k] for k in range(nb)], j)
        for k, copy in enumerate(scatter_a(j)):
            pack(slot(a_peers[k], b, c), 1, send_a.at[k], j)
            copy.start()

    def stage_5(j):
        if na:
            arrived(recv_a.at[:, :, :, wcols(j)], rr_sem.at[j, 0])
        merge(own_slot, 1, [recv_a.at[k] for k in range(na)], j, last=True)

    stages = (stage_0, stage_1, stage_2, stage_3, stage_4, stage_5)
    for number, j in ORDER:
        with jax.named_scope(f'st{number}_{j}'):
            stages[number](j)
    for k, (count, ref) in enumerate((
        (na, qall.at[pl.ds(0, na)]),
        (nb, qall.at[pl.ds(0, fa * nb)]),
        (nc, qall.at[pl.ds(0, fa * fb * nc)]),
        (na, send_a), (nb, send_b), (nc, send_c),
    )):
        if count:
            arrived(ref, send_sem.at[k])


def per_device(queries, new_keys, new_values, cache_keys, cache_values, victims):
    members = lax.axis_size("seq")
    dims = fa, fb, fc = factors(members)
    tok, columns = queries.shape
    heads = columns // HD
    sizes = chunks_of(heads)
    chunks = len(sizes)
    parts = len(GROUPS)
    rows = cache_keys.shape[0]
    keys = rows + -(-2 * tok // LANES) * LANES
    total = columns + chunks * LANES
    bf16 = jnp.bfloat16
    vmem = pl.BlockSpec(memory_space=pltpu.VMEM)
    hbm = pl.BlockSpec(memory_space=pl.ANY)
    return pl.pallas_call(
        functools.partial(kernel, dims, sizes),
        out_shape=pltpu.VMEM((tok, columns), bf16),
        in_specs=[hbm] * 6,
        out_specs=vmem,
        scratch_shapes=[
            pltpu.VMEM((tok, columns), bf16),
            pltpu.VMEM((tok, columns), bf16),
            pltpu.VMEM((1, victims.shape[0]), jnp.int32),
            pltpu.VMEM((members, tok, columns), bf16),
            pltpu.VMEM((keys, columns), bf16),
            pltpu.VMEM((keys, columns), bf16),
            pltpu.VMEM((keys, LANES), bf16),
            pltpu.VMEM((members, tok, total), jnp.float32),
            pltpu.VMEM((max(1, fc - 1), fa * fb, tok, total), bf16),
            pltpu.VMEM((max(1, fc - 1), fa * fb, tok, total), bf16),
            pltpu.VMEM((max(1, fb - 1), fa, tok, total), bf16),
            pltpu.VMEM((max(1, fb - 1), fa, tok, total), bf16),
            pltpu.VMEM((max(1, fa - 1), 1, tok, total), bf16),
            pltpu.VMEM((max(1, fa - 1), 1, tok, total), bf16),
            pltpu.SemaphoreType.DMA((2,)),
            pltpu.SemaphoreType.DMA((4,)),
            pltpu.SemaphoreType.DMA((6,)),
            pltpu.SemaphoreType.DMA((parts, max(1, fa - 1))),
            pltpu.SemaphoreType.DMA((parts, max(1, fb - 1))),
            pltpu.SemaphoreType.DMA((parts,)),
            pltpu.SemaphoreType.DMA((chunks, 3)),
        ],
        compiler_params=pltpu.CompilerParams(
            collective_id=0, has_side_effects=True, vmem_limit_bytes=60 * 1024 * 1024
        ),
    )(queries, new_keys, new_values, victims.reshape(1, -1), cache_keys, cache_values)


def solution(mesh):
    row = P(("groups", "seq"), None)
    return jax.shard_map(
        per_device,
        mesh=mesh,
        in_specs=(row, row, row, row, row, P("groups")),
        out_specs=row,
        check_vma=False,
    )
```

time: 30.5 us -> 27.2 us (0.89)
  Pallas kernels: 28.9 us -> 26.4 us
  local copies, waits for them, and re-layouts: 1.4 us -> 0.62 us
    pallas_call x1, Pallas kernels: 28.9 us -> 26.4 us  [per_device(): pl.pallas_call(functools.partial(kernel, dims, sizes), out_shape=pltpu.VM...]
    unnamed x1, local copies, waits for them, and re-layouts: 1.4 us -> 0.62 us
where the time goes in v1:
time: 27.2 us; the launch traced here: 27.1 us
  Pallas kernels  26.4 us (97%)
  local copies, waits for them, and re-layouts  0.62 us (2%)
    pallas_call x1, Pallas kernels, per_device(): pl.pallas_call(functools.partial(kernel, dims, sizes), out_shape=pltpu.VM...  26.4 us
    unnamed x1, local copies, waits for them, and re-layouts  0.62 us

profile of v1, /device:TPU:0, one launch (start us, length us, event | category | flops | bytes accessed | tf_op | source)
XLA Modules:
  0.0 27.1 jit_solution(14558719998799035206)
XLA Ops:
  0.0 26.4 %shard_map.64 = bf16[8,2560]{1,0:T(8,128)(2,1)S(1)} custom-call(bf16[8,2560]{1,0:T(8,128)(2,1)} %q_hbm.1, bf16[8,2560]{1,0:T(8,128)(2,1)} %nk_hbm.1, bf16[8,2560]{1,0:T(8,128)(2,1)} %nv_hbm.1, s32[1,16]{1,0:T(1,128)} %bitcast.1, bf16[512,2560]{1,0:T(8,128)(2,1)} %ck_ref.1, bf16[512,2560]{1,0:T(8,128)(2,1)} %cv_ref.1), custom_call_target="tpu_custom_call" | custom-call | tf_op jit(solution)/shard_map/pallas_call | solution.py:395
  26.5 0.6 %copy.8 = bf16[8,2560]{1,0:T(8,128)(2,1)} copy(bf16[8,2560]{1,0:T(8,128)(2,1)S(1)} %shard_map.64) | data formatting | bytes 81920

commit v2 on v1

--- a/solution.py
+++ b/solution.py
@@ -13,9 +13,7 @@
 LANES = 128
 HALF = 32
 ROW_TILE = 128
-SIZES = (4, 6, 6, 4)
-GROUPS = ((0, 1), (1, 2), (2, 4))
-ORDER = ((0, 0), (0, 1), (0, 2), (1, 0), (1, 1), (2, 0), (1, 2), (2, 1), (3, 0), (2, 2), (3, 1), (2, 3), (3, 2), (4, 0), (3, 3), (4, 1), (4, 2), (4, 3), (5, 0), (5, 1), (5, 2), (5, 3))
+CUTS = (0.15, 0.45, 0.8)
 
 
 def factors(members):
@@ -30,7 +28,34 @@
 
 
 def chunks_of(heads):
-    return SIZES
+    bounds = sorted({0, heads, *(round(heads * cut) for cut in CUTS)})
+    sizes = []
+    for low, high in zip(bounds, bounds[1:]):
+        while high - low > HALF:
+            sizes.append(HALF)
+            low += HALF
+        sizes.append(high - low)
+    return tuple(sizes)
+
+
+def groups_of(chunks):
+    bounds = sorted({0, min(1, chunks), min(2, chunks), chunks})
+    return tuple(zip(bounds, bounds[1:]))
+
+
+def order_of(chunks, groups):
+    order = [(0, g) for g in range(groups)] + [(1, g) for g in range(min(2, groups))]
+    for j in range(chunks):
+        order.append((2, j))
+        if j == 0:
+            order += [(1, g) for g in range(2, groups)]
+        else:
+            order.append((3, j - 1))
+    if chunks > 3:
+        order.append((4, 0))
+    order.append((3, chunks - 1))
+    order += [(4, j) for j in range(chunks) if (4, j) not in order]
+    return order + [(5, j) for j in range(chunks)]
 
 
 def kernel(
@@ -44,6 +69,7 @@
     heads = columns // HD
     chunks = len(sizes)
     starts = [sum(sizes[:j]) * HD for j in range(chunks + 1)]
+    groups = groups_of(chunks)
     rows = ck_ref.shape[0]
     keys = kbuf.shape[0]
     block_count = rows // BLK
@@ -87,7 +113,7 @@
     na, nb, nc = fa - 1, fb - 1, fc - 1
 
     def cols(g):
-        low, high = GROUPS[g]
+        low, high = groups[g]
         return pl.ds(starts[low], starts[high] - starts[low])
 
     def packed(j, h=0):
@@ -152,10 +178,9 @@
         src = qall.at[pl.ds(slot(0, at_b, c), fa), :, cols(j)]
         return [remote(src, src, 2, gc_sem.at[j], devices[na + nb + k]) for k in range(nc)]
 
-    with jax.named_scope('bar'):
-        own.wait()
-        pl.semaphore_wait(barrier, len(devices))
-    for j in range(len(GROUPS)):
+    own.wait()
+    pl.semaphore_wait(barrier, len(devices))
+    for j in range(len(groups)):
         for copy in gather_a(j):
             copy.start()
         for copy in gather_b(j, 0):
@@ -332,7 +357,7 @@
                 copy.start()
 
     def stage_2(j):
-        for g, (low, _) in enumerate(GROUPS):
+        for g, (low, _) in enumerate(groups):
             if nc and low == j:
                 arrived(qall.at[pl.ds(0, nc * fa * fb), :, cols(g)], gc_sem.at[g])
         compute(j)
@@ -340,21 +365,21 @@
             pack(slot(0, 0, c_peers[k]), fa * fb, send_c.at[k], j)
             copy.start()
 
+    def from_c(column):
+        return [recv_c.at[k, pl.ds(column * fa, fa)] for k in range(nc)]
+
     def stage_3(j):
         if nc:
             arrived(recv_c.at[:, :, :, wcols(j)], rr_sem.at[j, 2])
-        received = [recv_c.at[k] for k in range(nc)]
         for k, copy in enumerate(scatter_b(j)):
-            first = b_peers[k] * fa
-            merge(slot(0, b_peers[k], c), fa, [x.at[pl.ds(first, fa)] for x in received], j)
+            merge(slot(0, b_peers[k], c), fa, from_c(b_peers[k]), j)
             pack(slot(0, b_peers[k], c), fa, send_b.at[k], j)
             copy.start()
-        merge(slot(0, b, c), fa, [x.at[pl.ds(b * fa, fa)] for x in received], j)
 
     def stage_4(j):
         if nb:
             arrived(recv_b.at[:, :, :, wcols(j)], rr_sem.at[j, 1])
-        merge(slot(0, b, c), fa, [recv_b.at[k] for k in range(nb)], j)
+        merge(slot(0, b, c), fa, from_c(b) + [recv_b.at[k] for k in range(nb)], j)
         for k, copy in enumerate(scatter_a(j)):
             pack(slot(a_peers[k], b, c), 1, send_a.at[k], j)
             copy.start()
@@ -365,9 +390,8 @@
         merge(own_slot, 1, [recv_a.at[k] for k in range(na)], j, last=True)
 
     stages = (stage_0, stage_1, stage_2, stage_3, stage_4, stage_5)
-    for number, j in ORDER:
-        with jax.named_scope(f'st{number}_{j}'):
-            stages[number](j)
+    for number, j in order_of(chunks, len(groups)):
+        stages[number](j)
     for k, (count, ref) in enumerate((
         (na, qall.at[pl.ds(0, na)]),
         (nb, qall.at[pl.ds(0, fa * nb)]),
@@ -385,7 +409,7 @@
     heads = columns // HD
     sizes = chunks_of(heads)
     chunks = len(sizes)
-    parts = len(GROUPS)
+    parts = len(groups_of(chunks))
     rows = cache_keys.shape[0]
     keys = rows + -(-2 * tok // LANES) * LANES
     total = columns + chunks * LANES

time: 27.2 us -> 27.1 us (level)
  no operation moved by 1% of the time
where the time goes in v2:
time: 27.1 us; the launch traced here: 26.9 us
  Pallas kernels  26.3 us (97%)
  local copies, waits for them, and re-layouts  0.62 us (2%)
    pallas_call x1, Pallas kernels, per_device(): pl.pallas_call(functools.partial(kernel, dims, sizes), out_shape=pltpu.VM...  26.3 us
    unnamed x1, local copies, waits for them, and re-layouts  0.62 us

profile of v2, /device:TPU:0, one launch (start us, length us, event | category | flops | bytes accessed | tf_op | source)
XLA Modules:
  0.0 26.9 jit_solution(8496041783805792829)
XLA Ops:
  0.0 26.3 %shard_map.64 = bf16[8,2560]{1,0:T(8,128)(2,1)S(1)} custom-call(bf16[8,2560]{1,0:T(8,128)(2,1)} %q_hbm.1, bf16[8,2560]{1,0:T(8,128)(2,1)} %nk_hbm.1, bf16[8,2560]{1,0:T(8,128)(2,1)} %nv_hbm.1, s32[1,16]{1,0:T(1,128)} %bitcast.1, bf16[512,2560]{1,0:T(8,128)(2,1)} %ck_ref.1, bf16[512,2560]{1,0:T(8,128)(2,1)} %cv_ref.1), custom_call_target="tpu_custom_call" | custom-call | tf_op jit(solution)/shard_map/pallas_call | solution.py:419
  26.3 0.6 %copy.8 = bf16[8,2560]{1,0:T(8,128)(2,1)} copy(bf16[8,2560]{1,0:T(8,128)(2,1)S(1)} %shard_map.64) | data formatting | bytes 81920
